TPU v7x, 512 devices: a whole 4x4x16 slice. The times are simulated.
512 devices in a mesh: gx: 8 (over y, core), gy: 8 (over z_lo), gz: 8 (over x, z_hi).
Axes of the slice: x: 4, y: 4, z: 16 (z_hi: 2, z_lo: 8; z = z_hi * 8 + z_lo), core: 2. Of those that a mesh axis runs over, the one named last changes fastest.
Arguments:
- charges: float32 [8, 128, 128, 1024], P(None, 'gx', 'gy', 'gz'), may hold values from -120 to 120
- permittivity: float32 [128, 128, 1024], P('gx', 'gy', 'gz'), may hold values from 1 to 8
- screening: float32 [128, 128, 1024], P('gx', 'gy', 'gz'), may hold values from 0.05 to 2
Outputs:
- top_power: float32 [8, 128, 128, 1024], P(None, 'gx', 'gy', 'gz')
- r_factor: float32 [40, 40], replicated
All inputs are finite; a program needn't handle non-finite values.
Results may differ from a plain program's by a relative error of at most 0.0002.
Values sent between devices are 32-bit elements; how exact they have to be, the bound alone decides.
A program may use at most 64 MiB of HBM per device.

v0:
```python
import jax
import jax.numpy as jnp
from jax import lax
from jax.sharding import PartitionSpec as P

BASIS = 4
COLUMNS = 40


shift_value = 20.0
spread_value = 50.0


def extended(value, sides, width):
    for axis, dim in sides:
        peers, length = (lax.axis_size(axis), value.shape[dim])
        up = [(i, (i + 1) % peers) for i in range(peers - 1)]
        down = [(j, i) for i, j in up]
        last = lax.slice_in_dim(value, length - width, length, axis=dim)
        leading = lax.slice_in_dim(value, 0, width, axis=dim)
        before = lax.ppermute(last, axis, up)
        after = lax.ppermute(leading, axis, down)
        value = jnp.concatenate([before, value, after], axis=dim)
    return value


def apply_operator(padded, eps_pad, screen):
    centre = padded[:, 1:-1, 1:-1, 1:-1]
    eps_mid = eps_pad[1:-1, 1:-1, 1:-1]
    result_sum = screen * centre
    for dimension in range(3):
        length = eps_pad.shape[dimension] - 2
        for offset in (0, 2):
            index_list = [slice(1, -1), slice(1, -1), slice(1, -1)]
            index_list[dimension] = slice(offset, offset + length)
            neighbour = tuple(index_list)
            weight = 0.5 * (eps_mid + eps_pad[neighbour])
            result_sum = result_sum + weight * (centre - padded[(slice(None),) + neighbour])
    return (result_sum - shift_value * centre) / spread_value


def per_device(charges, permittivity, screening):
    brick_x, brick_y, brick_z = permittivity.shape
    count_x = lax.axis_size("gx")
    count_y = lax.axis_size("gy")
    count_z = lax.axis_size("gz")
    blocks = [charges]
    eps_pad = extended(permittivity, (("gx", 0), ("gy", 1), ("gz", 2)), 1)
    current_block = charges
    for power in range(BASIS):
        padded = extended(current_block, (("gx", 1), ("gy", 2), ("gz", 3)), 1)
        current_block = apply_operator(padded, eps_pad, screening)
        blocks.append(current_block)
    basis = jnp.concatenate(blocks, 0).reshape(COLUMNS, -1)
    cell_count = brick_x * brick_y * brick_z * count_x * count_y * count_z
    gram_local = (
        jnp.dot(basis, basis.T, precision=lax.Precision.HIGHEST, preferred_element_type=jnp.float32)
        / cell_count
    )
    gram_total = lax.psum(gram_local, ("gx", "gy", "gz"))
    r_factor = jnp.linalg.cholesky(gram_total).T
    return (current_block, r_factor)


def solution(mesh):
    placed = (P(None, "gx", "gy", "gz"), P("gx", "gy", "gz"), P("gx", "gy", "gz"))
    return jax.shard_map(
        per_device,
        mesh=mesh,
        in_specs=placed,
        out_specs=(P(None, "gx", "gy", "gz"), P()),
        check_vma=False,
    )
```

profile of v0, /device:TPU:1, one launch (start us, length us, event | category | flops | bytes accessed | tf_op | source)
XLA Modules:
  0.0 399.9 jit_solution(13282609257140268087)
XLA Ops:
  1.4 4.6 %collective-permute-start = (f32[1,16,128]{2,1,0:T(8,128)S(1)}, f32[1,16,128]{2,1,0:T(8,128)S(1)}, u32[]{:S(2)}, u32[]{:S(2)}) collective-permute-start(f32[1,16,128]{2,1,0:T(8,128)S(1)} %get-tuple-element.51), channel_id=1, source_target_pairs={{0,64},{64,128},{128,192},{192,256},{256,320},{320,384},{384,448},... | collective-permute-start | bytes 24584 | tf_op jit(solution)/shard_map/ppermute | solution.py:21
  6.0 5.6 %collective-permute-start.2 = (f32[1,16,128]{2,1,0:T(8,128)S(1)}, f32[1,16,128]{2,1,0:T(8,128)S(1)}, u32[]{:S(2)}, u32[]{:S(2)}) collective-permute-start(f32[1,16,128]{2,1,0:T(8,128)S(1)} %get-tuple-element.50), channel_id=1, source_target_pairs={{64,0},{128,64},{192,128},{256,192},{320,256},{384,320},{448,384},... | collective-permute-start | bytes 24584 | tf_op jit(solution)/shard_map/ppermute | solution.py:22
  24.4 4.3 %collective-permute-start.5 = (f32[8,18,1,128]{3,0,2,1:T(8,128)S(1)}, f32[8,18,1,128]{3,0,2,1:T(8,128)S(1)}, u32[]{:S(2)}, u32[]{:S(2)}) collective-permute-start(f32[8,18,1,128]{3,0,2,1:T(8,128)S(1)} %get-tuple-element.28), channel_id=1, source_target_pairs={{0,8},{8,16},{16,24},{24,32},{32,40},{40,48},{48,56},{1,9},{9,17},... | collective-permute-start | bytes 221192 | tf_op jit(solution)/shard_map/ppermute | solution.py:21
  31.4 15.9 %collective-permute-start.8 = (f32[18,18,1]{2,1,0:T(8,128)S(1)}, f32[18,18,1]{2,1,0:T(8,128)}, u32[]{:S(2)}, u32[]{:S(2)}) collective-permute-start(f32[18,18,1]{2,1,0:T(8,128)S(1)} %get-tuple-element.44), channel_id=1, source_target_pairs={{0,1},{1,2},{2,3},{3,4},{4,5},{5,6},{6,7},{8,9},{9,10},{10,11},{11... | collective-permute-start | bytes 3896 | tf_op jit(solution)/shard_map/ppermute | solution.py:21
  52.4 12.9 %collective-permute-start.9 = (f32[8,18,18,1]{2,0,3,1:T(8,128)S(1)}, f32[8,18,18,1]{2,0,3,1:T(8,128)}, u32[]{:S(2)}, u32[]{:S(2)}) collective-permute-start(f32[8,18,18,1]{2,0,3,1:T(8,128)S(1)} %copy.33), channel_id=1, source_target_pairs={{0,1},{1,2},{2,3},{3,4},{4,5},{5,6},{6,7},{8,9},{9,10},{10,11},{11... | collective-permute-start | bytes 31112 | tf_op jit(solution)/shard_map/ppermute | solution.py:21
  70.7 7.3 %collective-permute-done.9 = f32[8,18,18,1]{2,0,3,1:T(8,128)} collective-permute-done((f32[8,18,18,1]{2,0,3,1:T(8,128)S(1)}, f32[8,18,18,1]{2,0,3,1:T(8,128)}, u32[]{:S(2)}, u32[]{:S(2)}) %collective-permute-start.9) | collective-permute-done | bytes 10400 | tf_op jit(solution)/shard_map/ppermute | solution.py:21
  84.9 4.8 %constant_dynamic-update-slice_fusion.9 = (f32[40,16,16,128]{3,0,2,1:T(8,128)}, f32[8,16,16,128]{3,0,2,1:T(8,128)S(1)}) fusion(f32[40,16,16,128]{3,0,2,1:T(8,128)} %get-tuple-element.39, f32[8,16,16,128]{3,0,2,1:T(8,128)} %copy-done, f32[8,18,18,1]{3,0,2,1:T(8,128)} %copy.37, f32[8,18,1,128]{3,0,2,1:T(8,128)} %copy-done.16, ...), kind=kLoop, calls=%fused_computation.192 | loop fusion | flops 8388608 | bytes 6858880
  89.8 5.2 %collective-permute-start.12 = (f32[8,1,16,128]{3,0,2,1:T(8,128)S(1)}, f32[8,1,16,128]{3,0,2,1:T(8,128)S(1)}, u32[]{:S(2)}, u32[]{:S(2)}) collective-permute-start(f32[8,1,16,128]{3,0,2,1:T(8,128)S(1)} %get-tuple-element.34), channel_id=1, source_target_pairs={{0,64},{64,128},{128,192},{192,256},{256,320},{320,384},{384,448},... | collective-permute-start | bytes 196616 | tf_op jit(solution)/shard_map/ppermute | solution.py:21
  100.7 16.0 %collective-permute-start.14 = (f32[8,18,1,128]{3,0,2,1:T(8,128)S(1)}, f32[8,18,1,128]{3,0,2,1:T(8,128)S(1)}, u32[]{:S(2)}, u32[]{:S(2)}) collective-permute-start(f32[8,18,1,128]{3,0,2,1:T(8,128)S(1)} %get-tuple-element.26), channel_id=1, source_target_pairs={{0,8},{8,16},{16,24},{24,32},{32,40},{40,48},{48,56},{1,9},{9,17},... | collective-permute-start | bytes 221192 | tf_op jit(solution)/shard_map/ppermute | solution.py:21
  126.9 13.5 %collective-permute-start.16 = (f32[8,18,18,1]{2,0,3,1:T(8,128)}, f32[8,18,18,1]{2,0,3,1:T(8,128)}, u32[]{:S(2)}, u32[]{:S(2)}) collective-permute-start(f32[8,18,18,1]{2,0,3,1:T(8,128)} %copy.40), channel_id=1, source_target_pairs={{0,1},{1,2},{2,3},{3,4},{4,5},{5,6},{6,7},{8,9},{9,10},{10,11},{11... | collective-permute-start | bytes 31112 | tf_op jit(solution)/shard_map/ppermute | solution.py:21
  147.0 9.6 %collective-permute-done.17 = f32[8,18,18,1]{2,0,3,1:T(8,128)S(1)} collective-permute-done((f32[8,18,18,1]{2,0,3,1:T(8,128)}, f32[8,18,18,1]{2,0,3,1:T(8,128)S(1)}, u32[]{:S(2)}, u32[]{:S(2)}) %collective-permute-start.17) | collective-permute-done | bytes 10400 | tf_op jit(solution)/shard_map/ppermute | solution.py:22
  158.7 4.2 %constant_dynamic-update-slice_fusion.8 = (f32[40,16,16,128]{3,0,2,1:T(8,128)}, f32[8,16,16,128]{3,0,2,1:T(8,128)S(1)}) fusion(f32[40,16,16,128]{3,0,2,1:T(8,128)} %get-tuple-element.12, f32[8,16,16,128]{3,0,2,1:T(8,128)S(1)} %get-tuple-element.13, f32[8,16,16,128]{3,0,2,1:T(8,128)S(1)} %broadcast_multiply_fusion.2, f32[8,18,18,1]{3,0,2,1:T(8,128)} %copy.43, ...), kind=kLoop, calls=%fused_computation.191 | loop fusion | flops 10485760 | bytes 8044544
  163.1 4.9 %collective-permute-start.18 = (f32[8,1,16,128]{3,0,2,1:T(8,128)S(1)}, f32[8,1,16,128]{3,0,2,1:T(8,128)S(1)}, u32[]{:S(2)}, u32[]{:S(2)}) collective-permute-start(f32[8,1,16,128]{3,0,2,1:T(8,128)S(1)} %get-tuple-element.32), channel_id=1, source_target_pairs={{0,64},{64,128},{128,192},{192,256},{256,320},{320,384},{384,448},... | collective-permute-start | bytes 196616 | tf_op jit(solution)/shard_map/ppermute | solution.py:21
  186.4 4.5 %collective-permute-start.22 = (f32[8,18,18,1]{2,0,3,1:T(8,128)S(1)}, f32[8,18,18,1]{2,0,3,1:T(8,128)S(1)}, u32[]{:S(2)}, u32[]{:S(2)}) collective-permute-start(f32[8,18,18,1]{2,0,3,1:T(8,128)S(1)} %copy.44), channel_id=1, source_target_pairs={{0,1},{1,2},{2,3},{3,4},{4,5},{5,6},{6,7},{8,9},{9,10},{10,11},{11... | collective-permute-start | bytes 31112 | tf_op jit(solution)/shard_map/ppermute | solution.py:21
  196.8 12.4 %collective-permute-done.23 = f32[8,18,18,1]{2,0,3,1:T(8,128)S(1)} collective-permute-done((f32[8,18,18,1]{2,0,3,1:T(8,128)S(1)}, f32[8,18,18,1]{2,0,3,1:T(8,128)S(1)}, u32[]{:S(2)}, u32[]{:S(2)}) %collective-permute-start.23) | collective-permute-done | bytes 10400 | tf_op jit(solution)/shard_map/ppermute | solution.py:22
  211.2 4.2 %constant_dynamic-update-slice_fusion.7 = (f32[40,16,16,128]{3,0,2,1:T(8,128)}, f32[8,16,16,128]{3,0,2,1:T(8,128)S(1)}) fusion(f32[40,16,16,128]{3,0,2,1:T(8,128)} %get-tuple-element.10, f32[8,16,16,128]{3,0,2,1:T(8,128)S(1)} %get-tuple-element.11, f32[8,16,16,128]{3,0,2,1:T(8,128)S(1)} %broadcast_multiply_fusion.1, f32[8,18,18,1]{3,0,2,1:T(8,128)} %copy.47, ...), kind=kLoop, calls=%fused_computation.190 | loop fusion | flops 10485760 | bytes 8044544
  215.5 13.3 %collective-permute-start.24 = (f32[8,1,16,128]{3,0,2,1:T(8,128)S(1)}, f32[8,1,16,128]{3,0,2,1:T(8,128)S(1)}, u32[]{:S(2)}, u32[]{:S(2)}) collective-permute-start(f32[8,1,16,128]{3,0,2,1:T(8,128)S(1)} %get-tuple-element.30), channel_id=1, source_target_pairs={{0,64},{64,128},{128,192},{192,256},{256,320},{320,384},{384,448},... | collective-permute-start | bytes 196616 | tf_op jit(solution)/shard_map/ppermute | solution.py:21
  234.4 6.4 %collective-permute-start.26 = (f32[8,18,1,128]{3,0,2,1:T(8,128)S(1)}, f32[8,18,1,128]{3,0,2,1:T(8,128)S(1)}, u32[]{:S(2)}, u32[]{:S(2)}) collective-permute-start(f32[8,18,1,128]{3,0,2,1:T(8,128)S(1)} %get-tuple-element.22), channel_id=1, source_target_pairs={{0,8},{8,16},{16,24},{24,32},{32,40},{40,48},{48,56},{1,9},{9,17},... | collective-permute-start | bytes 221192 | tf_op jit(solution)/shard_map/ppermute | solution.py:21
  242.2 3.7 collective-permute-done.27
  251.0 4.8 %collective-permute-start.28 = (f32[8,18,18,1]{2,0,3,1:T(8,128)}, f32[8,18,18,1]{2,0,3,1:T(8,128)}, u32[]{:S(2)}, u32[]{:S(2)}) collective-permute-start(f32[8,18,18,1]{2,0,3,1:T(8,128)} %copy.48), channel_id=1, source_target_pairs={{0,1},{1,2},{2,3},{3,4},{4,5},{5,6},{6,7},{8,9},{9,10},{10,11},{11... | collective-permute-start | bytes 31112 | tf_op jit(solution)/shard_map/ppermute | solution.py:21
  260.7 11.3 %collective-permute-done.29 = f32[8,18,18,1]{2,0,3,1:T(8,128)} collective-permute-done((f32[8,18,18,1]{2,0,3,1:T(8,128)}, f32[8,18,18,1]{2,0,3,1:T(8,128)}, u32[]{:S(2)}, u32[]{:S(2)}) %collective-permute-start.29) | collective-permute-done | bytes 10400 | tf_op jit(solution)/shard_map/ppermute | solution.py:22
  275.0 4.2 %constant_dynamic-update-slice_fusion.6 = (f32[40,16,16,128]{3,0,2,1:T(8,128)}, f32[8,16,16,128]{3,0,2,1:T(8,128)}) fusion(f32[40,16,16,128]{3,0,2,1:T(8,128)} %get-tuple-element.8, f32[8,16,16,128]{3,0,2,1:T(8,128)S(1)} %get-tuple-element.9, f32[8,16,16,128]{3,0,2,1:T(8,128)S(1)} %broadcast_multiply_fusion, f32[8,18,18,1]{3,0,2,1:T(8,128)} %copy.51, ...), kind=kLoop, calls=%fused_computation.189 | loop fusion | flops 10485760 | bytes 6727808 | tf_op jit(solution)/shard_map/concatenate | solution.py:54
  279.2 8.4 %fusion = f32[40,40]{0,1:T(8,128)S(1)} fusion(f32[40,16,16,128]{3,0,2,1:T(8,128)} %get-tuple-element.6), kind=kOutput, calls=%fused_computation.5 | convolution fusion | flops 629147200 | bytes 5249280 | tf_op jit(solution)/shard_map/dot_general | solution.py:57
  287.6 105.3 %psum.7 = f32[40,40]{0,1:T(8,128)S(1)} all-reduce(f32[40,40]{0,1:T(8,128)S(1)} %fusion), channel_id=1, replica_groups=mesh['gx'=8,'gy'=8,'gz'=8] {'gx','gy','gz'}, use_global_device_ids=true, to_apply=%region_0.0 | all-reduce | flops 1600 | bytes 12800 | tf_op jit(solution)/shard_map/psum | solution.py:60
  (150 shorter events, 111.2 us)
Async XLA Ops:
  1.4 12.0 %collective-permute-start = (f32[1,16,128]{2,1,0:T(8,128)S(1)}, f32[1,16,128]{2,1,0:T(8,128)S(1)}, u32[]{:S(2)}, u32[]{:S(2)}) collective-permute-start(f32[1,16,128]{2,1,0:T(8,128)S(1)} %get-tuple-element.51), channel_id=1, source_target_pairs={{0,64},{64,128},{128,192},{192,256},{256,320},{320,384},{384,448},... | collective-permute-start | bytes 24584 | tf_op jit(solution)/shard_map/ppermute | solution.py:21
  6.0 7.5 %collective-permute-start.2 = (f32[1,16,128]{2,1,0:T(8,128)S(1)}, f32[1,16,128]{2,1,0:T(8,128)S(1)}, u32[]{:S(2)}, u32[]{:S(2)}) collective-permute-start(f32[1,16,128]{2,1,0:T(8,128)S(1)} %get-tuple-element.50), channel_id=1, source_target_pairs={{64,0},{128,64},{192,128},{256,192},{320,256},{384,320},{448,384},... | collective-permute-start | bytes 24584 | tf_op jit(solution)/shard_map/ppermute | solution.py:22
  13.5 7.2 %collective-permute-start.4 = (f32[18,1,128]{2,1,0:T(1,128)S(1)}, f32[18,1,128]{2,1,0:T(1,128)S(1)}, u32[]{:S(2)}, u32[]{:S(2)}) collective-permute-start(f32[18,1,128]{2,1,0:T(1,128)S(1)} %get-tuple-element.46), channel_id=1, source_target_pairs={{0,8},{8,16},{16,24},{24,32},{32,40},{40,48},{48,56},{1,9},{9,17},... | collective-permute-start | bytes 27656 | tf_op jit(solution)/shard_map/ppermute | solution.py:21
  14.8 5.9 %collective-permute-start.6 = (f32[18,1,128]{2,1,0:T(1,128)S(1)}, f32[18,1,128]{2,1,0:T(1,128)S(1)}, u32[]{:S(2)}, u32[]{:S(2)}) collective-permute-start(f32[18,1,128]{2,1,0:T(1,128)S(1)} %get-tuple-element.47), channel_id=1, source_target_pairs={{8,0},{16,8},{24,16},{32,24},{40,32},{48,40},{56,48},{9,1},{17,9},... | collective-permute-start | bytes 27656 | tf_op jit(solution)/shard_map/ppermute | solution.py:22
  18.8 5.6 %collective-permute-start.3 = (f32[8,1,16,128]{3,0,2,1:T(8,128)S(1)}, f32[8,1,16,128]{3,0,2,1:T(8,128)S(1)}, u32[]{:S(2)}, u32[]{:S(2)}) collective-permute-start(f32[8,1,16,128]{3,0,2,1:T(8,128)S(1)} %get-tuple-element.36), channel_id=1, source_target_pairs={{64,0},{128,64},{192,128},{256,192},{320,256},{384,320},{448,384},... | collective-permute-start | bytes 196616 | tf_op jit(solution)/shard_map/ppermute | solution.py:22
  24.4 22.9 %collective-permute-start.5 = (f32[8,18,1,128]{3,0,2,1:T(8,128)S(1)}, f32[8,18,1,128]{3,0,2,1:T(8,128)S(1)}, u32[]{:S(2)}, u32[]{:S(2)}) collective-permute-start(f32[8,18,1,128]{3,0,2,1:T(8,128)S(1)} %get-tuple-element.28), channel_id=1, source_target_pairs={{0,8},{8,16},{16,24},{24,32},{32,40},{40,48},{48,56},{1,9},{9,17},... | collective-permute-start | bytes 221192 | tf_op jit(solution)/shard_map/ppermute | solution.py:21
  28.7 18.6 %collective-permute-start.7 = (f32[8,18,1,128]{3,0,2,1:T(8,128)S(1)}, f32[8,18,1,128]{3,0,2,1:T(8,128)S(1)}, u32[]{:S(2)}, u32[]{:S(2)}) collective-permute-start(f32[8,18,1,128]{3,0,2,1:T(8,128)S(1)} %get-tuple-element.29), channel_id=1, source_target_pairs={{8,0},{16,8},{24,16},{32,24},{40,32},{48,40},{56,48},{9,1},{17,9},... | collective-permute-start | bytes 221192 | tf_op jit(solution)/shard_map/ppermute | solution.py:22
  30.1 38.1 %collective-permute-start.10 = (f32[18,18,1]{2,1,0:T(8,128)S(1)}, f32[18,18,1]{2,1,0:T(8,128)S(1)}, u32[]{:S(2)}, u32[]{:S(2)}) collective-permute-start(f32[18,18,1]{2,1,0:T(8,128)S(1)} %get-tuple-element.45), channel_id=1, source_target_pairs={{1,0},{2,1},{3,2},{4,3},{5,4},{6,5},{7,6},{9,8},{10,9},{11,10},{12... | collective-permute-start | bytes 3896 | tf_op jit(solution)/shard_map/ppermute | solution.py:22
  31.4 37.3 %collective-permute-start.8 = (f32[18,18,1]{2,1,0:T(8,128)S(1)}, f32[18,18,1]{2,1,0:T(8,128)}, u32[]{:S(2)}, u32[]{:S(2)}) collective-permute-start(f32[18,18,1]{2,1,0:T(8,128)S(1)} %get-tuple-element.44), channel_id=1, source_target_pairs={{0,1},{1,2},{2,3},{3,4},{4,5},{5,6},{6,7},{8,9},{9,10},{10,11},{11... | collective-permute-start | bytes 3896 | tf_op jit(solution)/shard_map/ppermute | solution.py:21
  52.4 25.6 %collective-permute-start.9 = (f32[8,18,18,1]{2,0,3,1:T(8,128)S(1)}, f32[8,18,18,1]{2,0,3,1:T(8,128)}, u32[]{:S(2)}, u32[]{:S(2)}) collective-permute-start(f32[8,18,18,1]{2,0,3,1:T(8,128)S(1)} %copy.33), channel_id=1, source_target_pairs={{0,1},{1,2},{2,3},{3,4},{4,5},{5,6},{6,7},{8,9},{9,10},{10,11},{11... | collective-permute-start | bytes 31112 | tf_op jit(solution)/shard_map/ppermute | solution.py:21
  66.9 15.9 %collective-permute-start.11 = (f32[8,18,18,1]{2,0,3,1:T(8,128)}, f32[8,18,18,1]{2,0,3,1:T(8,128)S(1)}, u32[]{:S(2)}, u32[]{:S(2)}) collective-permute-start(f32[8,18,18,1]{2,0,3,1:T(8,128)} %copy.36), channel_id=1, source_target_pairs={{1,0},{2,1},{3,2},{4,3},{5,4},{6,5},{7,6},{9,8},{10,9},{11,10},{12... | collective-permute-start | bytes 31112 | tf_op jit(solution)/shard_map/ppermute | solution.py:22
  89.8 7.1 %collective-permute-start.12 = (f32[8,1,16,128]{3,0,2,1:T(8,128)S(1)}, f32[8,1,16,128]{3,0,2,1:T(8,128)S(1)}, u32[]{:S(2)}, u32[]{:S(2)}) collective-permute-start(f32[8,1,16,128]{3,0,2,1:T(8,128)S(1)} %get-tuple-element.34), channel_id=1, source_target_pairs={{0,64},{64,128},{128,192},{192,256},{256,320},{320,384},{384,448},... | collective-permute-start | bytes 196616 | tf_op jit(solution)/shard_map/ppermute | solution.py:21
  95.1 5.6 %collective-permute-start.13 = (f32[8,1,16,128]{3,0,2,1:T(8,128)S(1)}, f32[8,1,16,128]{3,0,2,1:T(8,128)S(1)}, u32[]{:S(2)}, u32[]{:S(2)}) collective-permute-start(f32[8,1,16,128]{3,0,2,1:T(8,128)S(1)} %get-tuple-element.35), channel_id=1, source_target_pairs={{64,0},{128,64},{192,128},{256,192},{320,256},{384,320},{448,384},... | collective-permute-start | bytes 196616 | tf_op jit(solution)/shard_map/ppermute | solution.py:22
  100.7 17.4 %collective-permute-start.14 = (f32[8,18,1,128]{3,0,2,1:T(8,128)S(1)}, f32[8,18,1,128]{3,0,2,1:T(8,128)S(1)}, u32[]{:S(2)}, u32[]{:S(2)}) collective-permute-start(f32[8,18,1,128]{3,0,2,1:T(8,128)S(1)} %get-tuple-element.26), channel_id=1, source_target_pairs={{0,8},{8,16},{16,24},{24,32},{32,40},{40,48},{48,56},{1,9},{9,17},... | collective-permute-start | bytes 221192 | tf_op jit(solution)/shard_map/ppermute | solution.py:21
  126.9 17.1 %collective-permute-start.16 = (f32[8,18,18,1]{2,0,3,1:T(8,128)}, f32[8,18,18,1]{2,0,3,1:T(8,128)}, u32[]{:S(2)}, u32[]{:S(2)}) collective-permute-start(f32[8,18,18,1]{2,0,3,1:T(8,128)} %copy.40), channel_id=1, source_target_pairs={{0,1},{1,2},{2,3},{3,4},{4,5},{5,6},{6,7},{8,9},{9,10},{10,11},{11... | collective-permute-start | bytes 31112 | tf_op jit(solution)/shard_map/ppermute | solution.py:21
  142.0 14.6 %collective-permute-start.17 = (f32[8,18,18,1]{2,0,3,1:T(8,128)}, f32[8,18,18,1]{2,0,3,1:T(8,128)S(1)}, u32[]{:S(2)}, u32[]{:S(2)}) collective-permute-start(f32[8,18,18,1]{2,0,3,1:T(8,128)} %copy.42), channel_id=1, source_target_pairs={{1,0},{2,1},{3,2},{4,3},{5,4},{6,5},{7,6},{9,8},{10,9},{11,10},{12... | collective-permute-start | bytes 31112 | tf_op jit(solution)/shard_map/ppermute | solution.py:22
  163.1 6.8 %collective-permute-start.18 = (f32[8,1,16,128]{3,0,2,1:T(8,128)S(1)}, f32[8,1,16,128]{3,0,2,1:T(8,128)S(1)}, u32[]{:S(2)}, u32[]{:S(2)}) collective-permute-start(f32[8,1,16,128]{3,0,2,1:T(8,128)S(1)} %get-tuple-element.32), channel_id=1, source_target_pairs={{0,64},{64,128},{128,192},{192,256},{256,320},{320,384},{384,448},... | collective-permute-start | bytes 196616 | tf_op jit(solution)/shard_map/ppermute | solution.py:21
  167.9 5.6 %collective-permute-start.19 = (f32[8,1,16,128]{3,0,2,1:T(8,128)S(1)}, f32[8,1,16,128]{3,0,2,1:T(8,128)S(1)}, u32[]{:S(2)}, u32[]{:S(2)}) collective-permute-start(f32[8,1,16,128]{3,0,2,1:T(8,128)S(1)} %get-tuple-element.33), channel_id=1, source_target_pairs={{64,0},{128,64},{192,128},{256,192},{320,256},{384,320},{448,384},... | collective-permute-start | bytes 196616 | tf_op jit(solution)/shard_map/ppermute | solution.py:22
  186.4 8.2 %collective-permute-start.22 = (f32[8,18,18,1]{2,0,3,1:T(8,128)S(1)}, f32[8,18,18,1]{2,0,3,1:T(8,128)S(1)}, u32[]{:S(2)}, u32[]{:S(2)}) collective-permute-start(f32[8,18,18,1]{2,0,3,1:T(8,128)S(1)} %copy.44), channel_id=1, source_target_pairs={{0,1},{1,2},{2,3},{3,4},{4,5},{5,6},{6,7},{8,9},{9,10},{10,11},{11... | collective-permute-start | bytes 31112 | tf_op jit(solution)/shard_map/ppermute | solution.py:21
  193.2 15.9 %collective-permute-start.23 = (f32[8,18,18,1]{2,0,3,1:T(8,128)S(1)}, f32[8,18,18,1]{2,0,3,1:T(8,128)S(1)}, u32[]{:S(2)}, u32[]{:S(2)}) collective-permute-start(f32[8,18,18,1]{2,0,3,1:T(8,128)S(1)} %copy.46), channel_id=1, source_target_pairs={{1,0},{2,1},{3,2},{4,3},{5,4},{6,5},{7,6},{9,8},{10,9},{11,10},{12... | collective-permute-start | bytes 31112 | tf_op jit(solution)/shard_map/ppermute | solution.py:22
  215.5 15.3 %collective-permute-start.24 = (f32[8,1,16,128]{3,0,2,1:T(8,128)S(1)}, f32[8,1,16,128]{3,0,2,1:T(8,128)S(1)}, u32[]{:S(2)}, u32[]{:S(2)}) collective-permute-start(f32[8,1,16,128]{3,0,2,1:T(8,128)S(1)} %get-tuple-element.30), channel_id=1, source_target_pairs={{0,64},{64,128},{128,192},{192,256},{256,320},{320,384},{384,448},... | collective-permute-start | bytes 196616 | tf_op jit(solution)/shard_map/ppermute | solution.py:21
  234.4 7.8 %collective-permute-start.26 = (f32[8,18,1,128]{3,0,2,1:T(8,128)S(1)}, f32[8,18,1,128]{3,0,2,1:T(8,128)S(1)}, u32[]{:S(2)}, u32[]{:S(2)}) collective-permute-start(f32[8,18,1,128]{3,0,2,1:T(8,128)S(1)} %get-tuple-element.22), channel_id=1, source_target_pairs={{0,8},{8,16},{16,24},{24,32},{32,40},{40,48},{48,56},{1,9},{9,17},... | collective-permute-start | bytes 221192 | tf_op jit(solution)/shard_map/ppermute | solution.py:21
  251.0 7.8 %collective-permute-start.28 = (f32[8,18,18,1]{2,0,3,1:T(8,128)}, f32[8,18,18,1]{2,0,3,1:T(8,128)}, u32[]{:S(2)}, u32[]{:S(2)}) collective-permute-start(f32[8,18,18,1]{2,0,3,1:T(8,128)} %copy.48), channel_id=1, source_target_pairs={{0,1},{1,2},{2,3},{3,4},{4,5},{5,6},{6,7},{8,9},{9,10},{10,11},{11... | collective-permute-start | bytes 31112 | tf_op jit(solution)/shard_map/ppermute | solution.py:21
  257.4 14.7 %collective-permute-start.29 = (f32[8,18,18,1]{2,0,3,1:T(8,128)}, f32[8,18,18,1]{2,0,3,1:T(8,128)}, u32[]{:S(2)}, u32[]{:S(2)}) collective-permute-start(f32[8,18,18,1]{2,0,3,1:T(8,128)} %copy.50), channel_id=1, source_target_pairs={{1,0},{2,1},{3,2},{4,3},{5,4},{6,5},{7,6},{9,8},{10,9},{11,10},{12... | collective-permute-start | bytes 31112 | tf_op jit(solution)/shard_map/ppermute | solution.py:22
  (32 other events, 402.0 us)
where the time goes:
time: 401 us; the launch traced here: 400 us
  starting transfers between devices  140 us (35%)
  blocking collectives  105 us (26%)
  waiting for transfers between devices  67.5 us (17%)
  local copies, waits for them, and re-layouts  51.8 us (13%)
  other arithmetic  25.8 us (6%)
  matrix products  8.41 us (2%)
    ppermute x15, starting transfers between devices, extended(): before = lax.ppermute(last, axis, up)  113 us
    psum x1, blocking collectives, per_device(): gram_total = lax.psum(gram_local, ('gx', 'gy', 'gz'))  105 us
    ppermute x15, waiting for transfers between devices, extended(): after = lax.ppermute(leading, axis, down)  59.5 us
    ppermute x15, starting transfers between devices, extended(): after = lax.ppermute(leading, axis, down)  26.7 us
    slice x14, local copies, waits for them, and re-layouts, extended(): last = lax.slice_in_dim(value, length - width, length, axis=dim)  16.9 us
    unnamed x3, other arithmetic  13.2 us
    unnamed x59, local copies, waits for them, and re-layouts  9.19 us
    ppermute x4, local copies, waits for them, and re-layouts, extended(): after = lax.ppermute(leading, axis, down)  9.11 us
  transfers between devices with their start and end apart: 30, of which 15 were waited for; matrix products, arithmetic and copies ran while one was open for 6% of the time, Pallas kernels for 0%

commit v1 on v0

v1 whole, which is shorter than its diff:
```python
import functools

import jax
import jax.numpy as jnp
from jax import lax
from jax.experimental import pallas as pl
from jax.experimental.pallas import tpu as pltpu
from jax.sharding import PartitionSpec as P

MESH = pl.DeviceIdType.MESH
BASIS = 4
NRHS = 8
LANES = 128
MOMENTS = 2 * BASIS + 1
F32 = jnp.float32


def iota(dim):
    return lax.broadcasted_iota(jnp.int32, (8, LANES), dim)


def kernel(dims, ch, eps, scr, top, gram, p, ex, ey, eys, ezs, ezr, wgt, zs, zr, acc,
           sbuf, r1, r2, r3, ssem, rsem, esem, fsem, as1, ar1, as2, ar2, as3, ar3):
    bx, by, nx, ny, nz = dims
    per = LANES // by
    ix, iy, iz = (lax.axis_index(a) for a in ("gx", "gy", "gz"))
    zh = lax.rem(iz, 2)
    zx = lax.div(iz, 2)
    lane, row = iota(1), iota(0)

    faces = (
        (ix < nx - 1, (ix + 1, iy, iz), ix > 0),
        (ix > 0, (ix - 1, iy, iz), ix < nx - 1),
        (iy < ny - 1, (ix, iy + 1, iz), iy > 0),
        (iy > 0, (ix, iy - 1, iz), iy < ny - 1),
        (iz < nz - 1, (ix, iy, iz + 1), iz > 0),
        (iz > 0, (ix, iy, iz - 1), iz < nz - 1),
    )
    n3 = 2 * ny
    me3 = zh * ny + iy

    def peer1(d):
        j = lax.rem(ix + d, nx)
        return j, (j, iy, iz)

    def peer2(d):
        j = lax.rem(zx + d, nz // 2)
        return j, (ix, iy, 2 * j + zh)

    def peer3(d):
        j = lax.rem(me3 + d, n3)
        h = lax.div(j, ny)
        return j, (ix, j - h * ny, 2 * zx + h)

    barrier = pltpu.get_barrier_semaphore()
    count = jnp.int32(0)
    for out, peer, _ in faces:
        @pl.when(out)
        def _():
            pl.semaphore_signal(barrier, inc=1, device_id=peer, device_id_type=MESH)
        count = count + jnp.where(out, 1, 0)
    for n, peer in ((nx, peer1), (nz // 2, peer2), (n3, peer3)):
        @pl.loop(1, n)
        def _(d):
            pl.semaphore_signal(barrier, inc=1, device_id=peer(d)[1], device_id_type=MESH)
        count = count + (n - 1)

    zero = jnp.zeros((8, LANES), F32)

    @pl.loop(0, bx)
    def _(x):
        for y in range(by):
            p[0, x + 1, y + 1] = ch[pl.ds(x * by + y, 8, stride=bx * by), :]
        ex[x + 1] = eps[x]
        ey[x, pl.ds(8, by), :] = eps[x]
        eys[0, pl.ds(x, 1), :] = eps[x, pl.ds(0, 1), :]
        eys[1, pl.ds(x, 1), :] = eps[x, pl.ds(by - 1, 1), :]

    edge = jnp.zeros((by, LANES), F32)

    @pl.when(ix == 0)
    def _():
        ex[0] = edge

        @pl.loop(0, BASIS)
        def _(k):
            for y in range(by):
                p[k, 0, y + 1] = zero

    @pl.when(ix == nx - 1)
    def _():
        ex[bx + 1] = edge

        @pl.loop(0, BASIS)
        def _(k):
            for y in range(by):
                p[k, bx + 1, y + 1] = zero

    @pl.when(iy == 0)
    def _():
        ey[pl.ds(bx, 1)] = jnp.zeros((1, by + 16, LANES), F32)

        @pl.loop(0, BASIS)
        def _(k):
            for x in range(bx):
                p[k, x + 1, 0] = zero

    @pl.when(iy == ny - 1)
    def _():
        ey[pl.ds(bx + 1, 1)] = jnp.zeros((1, by + 16, LANES), F32)

        @pl.loop(0, BASIS)
        def _(k):
            for x in range(bx):
                p[k, x + 1, by + 1] = zero

    @pl.when(iz == 0)
    def _():
        ezr[0] = edge
        zr[:, 0] = jnp.zeros_like(zr[:, 0])

    @pl.when(iz == nz - 1)
    def _():
        ezr[1] = edge
        zr[:, 1] = jnp.zeros_like(zr[:, 1])

    lane_e = lax.broadcasted_iota(jnp.int32, (by, LANES), 1)
    ezs[...] = jnp.zeros_like(ezs)

    @pl.loop(0, bx)
    def _(x):
        e = eps[x]
        ezs[0] = jnp.where(lane_e == x, pltpu.roll(e, x, 1), ezs[0])
        ezs[1] = jnp.where(lane_e == x, pltpu.roll(e, x + 1, 1), ezs[1])

    def pack(k):
        @pl.loop(0, bx)
        def _(x):
            half = lax.div(x, per)
            shift = lax.rem(x, per) * by
            lo = hi = zero
            for y in range(by):
                v = p[k, x + 1, y + 1]
                lo = jnp.where(lane == y, pltpu.roll(v, y, 1), lo)
                hi = jnp.where(lane == y, pltpu.roll(v, y + 1, 1), hi)
            here = (lane >= shift) & (lane < shift + by)
            zs[k, 0, half] = jnp.where(here, pltpu.roll(lo, shift, 1), zs[k, 0, half])
            zs[k, 1, half] = jnp.where(here, pltpu.roll(hi, shift, 1), zs[k, 1, half])

    zs[...] = jnp.zeros_like(zs)
    pack(0)

    pl.semaphore_wait(barrier, count)

    def field(k, i):
        src, dst = (
            (p.at[k, bx, pl.ds(1, by)], p.at[k, 0, pl.ds(1, by)]),
            (p.at[k, 1, pl.ds(1, by)], p.at[k, bx + 1, pl.ds(1, by)]),
            (p.at[k, pl.ds(1, bx), by], p.at[k, pl.ds(1, bx), 0]),
            (p.at[k, pl.ds(1, bx), 1], p.at[k, pl.ds(1, bx), by + 1]),
            (zs.at[k, 1], zr.at[k, 0]),
            (zs.at[k, 0], zr.at[k, 1]),
        )[i]
        return pltpu.make_async_remote_copy(
            src_ref=src, dst_ref=dst, send_sem=ssem.at[k, i], recv_sem=rsem.at[k, i],
            device_id=faces[i][1], device_id_type=MESH)

    def coefficient(i):
        src, dst = (
            (ex.at[bx], ex.at[0]),
            (ex.at[1], ex.at[bx + 1]),
            (eys.at[1], ey.at[bx, pl.ds(8, bx)]),
            (eys.at[0], ey.at[bx + 1, pl.ds(8, bx)]),
            (ezs.at[1], ezr.at[0]),
            (ezs.at[0], ezr.at[1]),
        )[i]
        return pltpu.make_async_remote_copy(
            src_ref=src, dst_ref=dst, send_sem=esem.at[i], recv_sem=fsem.at[i],
            device_id=faces[i][1], device_id_type=MESH)

    def start(copies):
        for i in (4, 5, 0, 1, 2, 3):
            @pl.when(faces[i][0])
            def _():
                copies(i).start()

    def arrive(copies):
        for i in range(6):
            @pl.when(faces[i][2])
            def _():
                copies(i).wait_recv()

    def sent(copies):
        for i in range(6):
            @pl.when(faces[i][0])
            def _():
                copies(i).wait_send()

    start(functools.partial(field, 0))
    start(coefficient)

    def moments(k, first):
        def body(x, sums):
            sums = list(sums)
            for y in range(by):
                b = p[k, x + 1, y + 1]
                a = None if first else p[k - 1, x + 1, y + 1]
                for s in range(5):
                    t = b if s == 0 else pltpu.roll(b, s, 0)
                    sums[s] = sums[s] + b * t
                    if not first:
                        sums[5 + s] = sums[5 + s] + a * t
            return tuple(sums)
        sums = lax.fori_loop(0, bx, body, (zero,) * (5 if first else 10))
        for s in range(5):
            acc[2 * k, s] = sums[s]
            if not first:
                acc[2 * k - 1, s] = sums[5 + s]

    moments(0, True)
    arrive(coefficient)

    @pl.loop(0, bx)
    def _(x):
        e = eps[x]
        ey[x, pl.ds(0, 8), :] = jnp.broadcast_to(ey[bx, pl.ds(8 + x, 1), :], (8, LANES))
        ey[x, pl.ds(8 + by, 8), :] = jnp.broadcast_to(ey[bx + 1, pl.ds(8 + x, 1), :], (8, LANES))
        zm = jnp.where(lane_e == 0, pltpu.roll(ezr[0], lax.rem(LANES - x, LANES), 1), pltpu.roll(e, 1, 1))
        zp = jnp.where(lane_e == LANES - 1, pltpu.roll(ezr[1], LANES - 1 - x, 1), pltpu.roll(e, LANES - 1, 1))
        total = scr[x] * 0.02 - 0.4
        near = (ex[x], ex[x + 2], ey[x, pl.ds(7, by), :], ey[x, pl.ds(9, by), :], zm, zp)
        for i, n in enumerate(near):
            w = (e + n) * 0.01
            wgt[i, x] = w
            total = total + w
        wgt[6, x] = total

    @pl.loop(0, BASIS)
    def _(k):
        arrive(functools.partial(field, k))

        @pl.loop(0, bx)
        def _(x):
            shift = lax.rem(x, per) * by
            half = lax.div(x, per)
            lo = pltpu.roll(zr[k, 0, half], lax.rem(LANES - shift, LANES), 1)
            hi = pltpu.roll(zr[k, 1, half], LANES - 1 - shift, 1)
            for y in range(by):
                v = p[k, x + 1, y + 1]
                zm = jnp.where(lane == 0, pltpu.roll(lo, (LANES - y) % LANES, 1), pltpu.roll(v, 1, 1))
                zp = jnp.where(lane == LANES - 1, pltpu.roll(hi, (LANES - y) % LANES, 1), pltpu.roll(v, LANES - 1, 1))
                near = (p[k, x, y + 1], p[k, x + 2, y + 1], p[k, x + 1, y], p[k, x + 1, y + 2], zm, zp)
                w = [jnp.broadcast_to(wgt[i, x, pl.ds(y, 1), :], (8, LANES)) for i in range(7)]
                terms = [w[i] * near[i] for i in range(6)]
                p[k + 1, x + 1, y + 1] = w[6] * v - (((terms[0] + terms[1]) + (terms[2] + terms[3])) + (terms[4] + terms[5]))

        @pl.when(k < BASIS - 1)
        def _():
            pack(k + 1)
            start(functools.partial(field, k + 1))

        moments(k + 1, False)
        sent(functools.partial(field, k))

    sent(coefficient)

    def body(m, s_all):
        for s in range(8):
            part = acc[m, s] if s <= 4 else pltpu.roll(acc[m, 8 - s], s, 0)
            col = jnp.sum(part, axis=1, keepdims=True)
            s_all = jnp.where(lane == 8 * m + ((row - s) & 7), col, s_all)
        return s_all

    total = lax.fori_loop(0, MOMENTS, body, zero)

    for stage, (n, peer, me, slots, send, recv) in enumerate((
        (nx, peer1, ix, r1, as1, ar1), (nz // 2, peer2, zx, r2, as2, ar2), (n3, peer3, me3, r3, as3, ar3))):
        sbuf[stage] = total
        slots[me] = total

        def copy(d, mine):
            j, device = peer(d)
            return pltpu.make_async_remote_copy(
                src_ref=sbuf.at[stage], dst_ref=slots.at[me if mine else j], send_sem=send.at[d],
                recv_sem=recv.at[me if mine else j], device_id=device, device_id_type=MESH)

        @pl.loop(1, n)
        def _(d):
            copy(d, True).start()

        if stage == 0:
            @pl.loop(0, bx)
            def _(x):
                for y in range(by):
                    top[pl.ds(x * by + y, 8, stride=bx * by), :] = p[BASIS, x + 1, y + 1]

        @pl.loop(1, n)
        def _(d):
            copy(d, False).wait_recv()
        parts = [slots[j] for j in range(n)]
        while len(parts) > 1:
            parts = [parts[i] + parts[i + 1] for i in range(0, len(parts) - 1, 2)] + ([parts[-1]] if len(parts) % 2 else [])
        total = parts[0]

        @pl.loop(1, n)
        def _(d):
            copy(d, True).wait_send()

    cells = bx * by * LANES * nx * ny * nz
    total = total * (1.0 / cells)
    for i in range(BASIS + 1):
        gram[pl.ds(8 * i, 8), :] = total if i == 0 else pltpu.roll(total, LANES - 8 * i, 1)


def per_device(sizes, charges, permittivity, screening):
    _, bx, by, bz = charges.shape
    nx, ny, nz = sizes
    dims = (bx, by, nx, ny, nz)
    halves = max(1, bx * by // LANES)
    vmem = pl.BlockSpec(memory_space=pltpu.VMEM)
    dma = pltpu.SemaphoreType.DMA
    top, gram = pl.pallas_call(
        functools.partial(kernel, dims),
        out_shape=(
            jax.ShapeDtypeStruct((NRHS * bx * by, bz), F32),
            jax.ShapeDtypeStruct((8 * (BASIS + 1), LANES), F32),
        ),
        in_specs=[vmem] * 3,
        out_specs=(vmem, vmem),
        scratch_shapes=[
            pltpu.VMEM((BASIS + 1, bx + 2, by + 2, 8, LANES), F32),
            pltpu.VMEM((bx + 2, by, LANES), F32),
            pltpu.VMEM((bx + 2, by + 16, LANES), F32),
            pltpu.VMEM((2, bx, LANES), F32),
            pltpu.VMEM((2, by, LANES), F32),
            pltpu.VMEM((2, by, LANES), F32),
            pltpu.VMEM((7, bx, by, LANES), F32),
            pltpu.VMEM((BASIS, 2, halves, 8, LANES), F32),
            pltpu.VMEM((BASIS, 2, halves, 8, LANES), F32),
            pltpu.VMEM((MOMENTS, 5, 8, LANES), F32),
            pltpu.VMEM((3, 8, LANES), F32),
            pltpu.VMEM((nx, 8, LANES), F32),
            pltpu.VMEM((nz // 2, 8, LANES), F32),
            pltpu.VMEM((2 * ny, 8, LANES), F32),
            dma((BASIS, 6)), dma((BASIS, 6)), dma((6,)), dma((6,)),
            dma((nx,)), dma((nx,)), dma((nz // 2,)), dma((nz // 2,)), dma((2 * ny,)), dma((2 * ny,)),
        ],
        compiler_params=pltpu.CompilerParams(collective_id=0, has_side_effects=True),
    )(charges.reshape(NRHS * bx * by, bz), permittivity, screening)
    columns = NRHS * (BASIS + 1)
    r_factor = jnp.linalg.cholesky(gram[:, :columns]).T
    return top.reshape(NRHS, bx, by, bz), r_factor


def solution(mesh):
    sizes = tuple(mesh.shape[a] for a in ("gx", "gy", "gz"))
    placed = (P(None, "gx", "gy", "gz"), P("gx", "gy", "gz"), P("gx", "gy", "gz"))
    return jax.shard_map(
        functools.partial(per_device, sizes),
        mesh=mesh,
        in_specs=placed,
        out_specs=(P(None, "gx", "gy", "gz"), P()),
        check_vma=False,
    )
```

time: 401 us -> 100 us (0.25)
  starting transfers between devices: 140 us -> 0 us
  blocking collectives: 105 us -> 0 us
  Pallas kernels: 0 us -> 90.7 us
  waiting for transfers between devices: 67.5 us -> 0 us
  local copies, waits for them, and re-layouts: 51.8 us -> 3.85 us
  other arithmetic: 25.8 us -> 4.98 us
  matrix products: 8.41 us -> 0 us
    ppermute x30 -> x0, starting transfers between devices: 140 us -> none  [the longest x15 113 us: extended(): before = lax.ppermute(last, axis, up)]
    psum x1 -> x0, blocking collectives: 105 us -> none  [per_device(): gram_total = lax.psum(gram_local, ('gx', 'gy', 'gz'))]
    pallas_call x0 -> x1, Pallas kernels: none -> 90.7 us  [per_device(): pl.pallas_call(functools.partial(kernel, dims), out_shape=(jax.ShapeDtype...]
    ppermute x30 -> x0, waiting for transfers between devices: 67.5 us -> none  [the longest x15 59.5 us: extended(): after = lax.ppermute(leading, axis, down)]
    slice x20 -> x2, local copies, waits for them, and re-layouts: 24.6 us -> 0.08 us  [per_device(): r_factor = jnp.linalg.cholesky(gram[:, :columns]).T]
    ppermute x8 -> x0, local copies, waits for them, and re-layouts: 17.9 us -> none  [the longest x4 9.11 us: extended(): after = lax.ppermute(leading, axis, down)]
    unnamed x3 -> x0, other arithmetic: 13.2 us -> none
    dot_general x1 -> x0, matrix products: 8.41 us -> none  [per_device(): jnp.dot(basis, basis.T, precision=lax.Precision.HIGHEST, preferred_elemen...]
  transfers between devices with their start and end apart: 30 -> 0, of which waited for: 15 -> 0; matrix products, arithmetic and copies ran while one was open for 6% -> 0% of each run, Pallas kernels for 0% -> 0%
where the time goes in v1:
time: 100 us
  Pallas kernels  90.7 us (91%)
  other arithmetic  4.98 us (5%)
  local copies, waits for them, and re-layouts  3.85 us (4%)
    pallas_call x1, Pallas kernels, per_device(): pl.pallas_call(functools.partial(kernel, dims), out_shape=(jax.ShapeDtype...  90.7 us
    another operation x3, other arithmetic, per_device(): r_factor = jnp.linalg.cholesky(gram[:, :columns]).T  4.33 us
    unnamed x2, local copies, waits for them, and re-layouts  2.95 us

profile of v1, /device:TPU:1, one launch (start us, length us, event | category | flops | bytes accessed | tf_op | source)
XLA Modules:
  0.0 100.2 jit_solution(15714622843041464843)
XLA Ops:
  0.6 90.7 %shard_map.50 = (f32[2048,128]{1,0:T(8,128)}, f32[40,128]{1,0:T(8,128)}) custom-call(f32[2048,128]{1,0:T(8,128)} %bitcast.8, f32[16,16,128]{2,1,0:T(8,128)} %eps.1, f32[16,16,128]{2,1,0:T(8,128)} %scr.1), custom_call_target="tpu_custom_call" | custom-call | tf_op jit(solution)/shard_map/pallas_call | solution.py:322
  91.3 0.8 copy.5
  92.2 0.1 copy.6
  92.3 3.6 %cholesky.18 = f32[40,40]{1,0:T(8,128)S(1)} custom-call(f32[40,40]{1,0:T(8,128)S(1)} %fusion), custom_call_target="Cholesky" | custom-call | tf_op jit(solution)/shard_map/jit(cholesky)/cholesky | solution.py:351
  95.9 0.6 compare_reduce_fusion
  96.6 0.7 select_bitcast_fusion
  97.3 0.7 copy.7
  97.9 2.3 %copy.9 = f32[8,16,16,128]{3,2,1,0:T(8,128)} copy(f32[8,16,16,128]{3,2,1,0:T(8,128)} %bitcast.9) | data formatting | bytes 2097152
  (3 shorter events, 0.0 us)

commit v2 on v1

v2 whole, which is shorter than its diff:
```python
import functools

import jax
import jax.numpy as jnp
from jax import lax
from jax.experimental import pallas as pl
from jax.experimental.pallas import tpu as pltpu
from jax.sharding import PartitionSpec as P

MESH = pl.DeviceIdType.MESH
BASIS = 4
NRHS = 8
LANES = 128
MOMENTS = 2 * BASIS + 1
F32 = jnp.float32


def iota(dim):
    return lax.broadcasted_iota(jnp.int32, (8, LANES), dim)


def kernel(dims, ch, eps, scr, top, gram, p, ex, ey, eys, wgt, e, inj, yes, yer, sup, rup,
           ce, ie, csend, crecv, ees, eer, wge, acc, sbuf, r1, r2, r3,
           ssem, rsem, xsem, ysem, zsem, tsem, usem, vsem, esem, fsem, gsem, hsem,
           as1, ar1, as2, ar2, as3, ar3):
    bx, by, nx, ny, nz = dims
    ix, iy, iz = (lax.axis_index(a) for a in ("gx", "gy", "gz"))
    zh = lax.rem(iz, 2)
    zx = lax.div(iz, 2)
    lane, row = iota(1), iota(0)
    place = lane & 7
    zero = jnp.zeros((8, LANES), F32)

    faces = (
        (ix < nx - 1, (ix + 1, iy, iz), ix > 0),
        (ix > 0, (ix - 1, iy, iz), ix < nx - 1),
        (iy < ny - 1, (ix, iy + 1, iz), iy > 0),
        (iy > 0, (ix, iy - 1, iz), iy < ny - 1),
        (iz < nz - 1, (ix, iy, iz + 1), iz > 0),
        (iz > 0, (ix, iy, iz - 1), iz < nz - 1),
    )
    n3 = 2 * ny
    me3 = zh * ny + iy

    def peer1(d):
        j = lax.rem(ix + d, nx)
        return j, (j, iy, iz)

    def peer2(d):
        j = lax.rem(zx + d, nz // 2)
        return j, (ix, iy, 2 * j + zh)

    def peer3(d):
        j = lax.rem(me3 + d, n3)
        h = lax.div(j, ny)
        return j, (ix, j - h * ny, 2 * zx + h)

    barrier = pltpu.get_barrier_semaphore()
    count = jnp.int32(0)
    for out, peer, _ in faces:
        @pl.when(out)
        def _():
            pl.semaphore_signal(barrier, inc=1, device_id=peer, device_id_type=MESH)
        count = count + jnp.where(out, 1, 0)
    for n, peer in ((nx, peer1), (nz // 2, peer2), (n3, peer3)):
        @pl.loop(1, n)
        def _(d):
            pl.semaphore_signal(barrier, inc=1, device_id=peer(d)[1], device_id_type=MESH)
        count = count + (n - 1)

    def inject(y):
        return (lane == (8 * y + 8) % LANES) | (lane == (8 * y - 1) % LANES)

    @pl.loop(0, bx)
    def _(x):
        border, beyond = zero, zero
        for y in range(by):
            v = ch[pl.ds(x * by + y, 8, stride=bx * by), :]
            p[0, x + 1, y + 1] = v
            v = pltpu.roll(v, (8 * y + 4) % LANES, 1)
            border = jnp.where((lane >> 3) == y, v, border)
            beyond = jnp.where(inject(y), v, beyond)
        e[0, x + 1, 0] = border
        e[0, x + 1, 1] = border
        inj[0, x] = beyond
        ex[x + 1] = eps[pl.ds(x * by, by), :]
        ey[x, pl.ds(8, by), :] = eps[pl.ds(x * by, by), :]
        eys[0, pl.ds(x, 1), :] = eps[pl.ds(x * by, 1), :]
        eys[1, pl.ds(x, 1), :] = eps[pl.ds(x * by + by - 1, 1), :]

    @pl.loop(0, bx // 2)
    def _(j):
        even, odd = e[0, 2 * j + 1, 0], e[0, 2 * j + 2, 0]
        sup[0, j] = jnp.where(place < 4, even, pltpu.roll(odd, 4, 1))
        sup[1, j] = jnp.where(place < 4, pltpu.roll(even, LANES - 4, 1), odd)

    lane_e = lax.broadcasted_iota(jnp.int32, (bx, LANES), 1)
    row_e = lax.broadcasted_iota(jnp.int32, (bx, LANES), 0)
    place_e = lane_e & 7
    blank = jnp.zeros((bx, LANES), F32)
    c_e, c_s, i_e = blank, blank, blank
    for y in range(by):
        v = pltpu.roll(eps[pl.ds(y, bx, stride=by), :], (8 * y + 4) % LANES, 1)
        u = pltpu.roll(scr[pl.ds(y, bx, stride=by), :], (8 * y + 4) % LANES, 1)
        c_e = jnp.where((lane_e >> 3) == y, v, c_e)
        c_s = jnp.where((lane_e >> 3) == y, u, c_s)
        i_e = jnp.where((lane_e == (8 * y + 8) % LANES) | (lane_e == (8 * y - 1) % LANES), v, i_e)
    ce[0] = c_e
    ce[1] = c_s
    ie[...] = i_e
    csend[0] = jnp.where(place_e < 4, c_e, pltpu.roll(c_s, 4, 1))
    csend[1] = jnp.where(place_e < 4, pltpu.roll(c_s, LANES - 4, 1), c_e)

    edge = jnp.zeros((by, LANES), F32)
    for there, at, ghost in ((ix == 0, 0, 0), (ix == nx - 1, bx + 1, 1)):
        @pl.when(there)
        def _():
            ex[at] = edge
            for side in range(2):
                eer[ghost, side] = blank

            @pl.loop(0, BASIS)
            def _(k):
                for y in range(by):
                    p[k, at, y + 1] = zero
                e[k, at, 0] = zero
                e[k, at, 1] = zero

    for there, at, ghost in ((iy == 0, 0, 0), (iy == ny - 1, by + 1, 1)):
        @pl.when(there)
        def _():
            ey[pl.ds(bx + ghost, 1)] = jnp.zeros((1, by + 16, LANES), F32)
            for side in range(2):
                eer[2 + ghost, side] = blank

            @pl.loop(0, BASIS)
            def _(k):
                for x in range(bx):
                    p[k, x + 1, at] = zero
                yer[k, ghost, 0] = zero
                yer[k, ghost, 1] = zero

    for there, ghost in ((iz == 0, 0), (iz == nz - 1, 1)):
        @pl.when(there)
        def _():
            crecv[ghost] = blank
            for j in range(bx // 2):
                rup[ghost, j] = zero

    pl.semaphore_wait(barrier, count)

    def remote(src, dst, send, recv, i):
        return pltpu.make_async_remote_copy(
            src_ref=src, dst_ref=dst, send_sem=send, recv_sem=recv, device_id=faces[i][1], device_id_type=MESH)

    def field(k):
        pairs = (
            (p.at[k, bx, pl.ds(1, by)], p.at[k, 0, pl.ds(1, by)]),
            (p.at[k, 1, pl.ds(1, by)], p.at[k, bx + 1, pl.ds(1, by)]),
            (p.at[k, pl.ds(1, bx), by], p.at[k, pl.ds(1, bx), 0]),
            (p.at[k, pl.ds(1, bx), 1], p.at[k, pl.ds(1, bx), by + 1]),
        )
        return [(i, remote(*pairs[i], ssem.at[k, i], rsem.at[k, i], i)) for i in range(4)]

    def rim(k):
        pairs = (
            (e.at[k, bx], e.at[k, 0]),
            (e.at[k, 1], e.at[k, bx + 1]),
            (yes.at[k, 1], yer.at[k, 0]),
            (yes.at[k, 0], yer.at[k, 1]),
        )
        return [(i, remote(*pairs[i], xsem.at[k, i], ysem.at[k, i], i)) for i in range(4)]

    def far():
        return [(4 + i, remote(sup.at[i], rup.at[i], zsem.at[i], tsem.at[i], 4 + i)) for i in range(2)]

    def far_coefficient():
        return [(4 + i, remote(csend.at[i], crecv.at[i], usem.at[i], vsem.at[i], 4 + i)) for i in range(2)]

    def coefficient():
        pairs = (
            (ex.at[bx], ex.at[0]),
            (ex.at[1], ex.at[bx + 1]),
            (eys.at[1], ey.at[bx, pl.ds(8, bx)]),
            (eys.at[0], ey.at[bx + 1, pl.ds(8, bx)]),
        )
        return [(i, remote(*pairs[i], esem.at[i], fsem.at[i], i)) for i in range(4)]

    def rim_coefficient():
        return [(i, remote(ees, eer.at[i], gsem.at[i], hsem.at[i], i)) for i in range(4)]

    def start(copies):
        for i, c in copies:
            @pl.when(faces[i][0])
            def _():
                c.start()

    def arrive(copies):
        for i, c in copies:
            @pl.when(faces[i][2])
            def _():
                c.wait_recv()

    def sent(copies):
        for i, c in copies:
            @pl.when(faces[i][0])
            def _():
                c.wait_send()

    def moments(k):
        inner = (lane >= BASIS) & (lane < LANES - BASIS)

        def body(x, sums):
            sums = list(sums)
            for y in range(by):
                b = p[k, x + 1, y + 1]
                b = jnp.where(inner, b, 0.0)
                for s in range(5):
                    t = b if s == 0 else pltpu.roll(b, s, 0)
                    sums[s] = sums[s] + b * t
                    if k > 0:
                        sums[5 + s] = sums[5 + s] + p[k - 1, x + 1, y + 1] * t
            return tuple(sums)

        sums = lax.fori_loop(0, bx, body, (zero,) * (10 if k else 5))
        for s in range(5):
            acc[2 * k, s] = sums[s]
            if k > 0:
                acc[2 * k - 1, s] = sums[5 + s]

    def rim_moments(k):
        sums = [acc[2 * k, s] for s in range(5)] + ([acc[2 * k - 1, s] for s in range(5)] if k else [])
        for x in range(bx):
            b = jnp.where(place < 4, e[k, x + 1, 1], e[k, x + 1, 0])
            a = jnp.where(place < 4, e[k - 1, x + 1, 1], e[k - 1, x + 1, 0]) if k else None
            for s in range(5):
                t = b if s == 0 else pltpu.roll(b, s, 0)
                sums[s] = sums[s] + b * t
                if k > 0:
                    sums[5 + s] = sums[5 + s] + a * t
        for s in range(5):
            acc[2 * k, s] = sums[s]
            if k > 0:
                acc[2 * k - 1, s] = sums[5 + s]

    def reduce(first, last, table):
        for m in range(first, last):
            for s in range(8):
                part = acc[m, s] if s <= 4 else pltpu.roll(acc[m, 8 - s], s, 0)
                col = jnp.sum(part, axis=1, keepdims=True)
                table = jnp.where(lane == 8 * m + ((row - s) & 7), col, table)
        return table

    def spread(ref, *at):
        return jnp.broadcast_to(ref[at], (8, LANES))

    def step(k):
        @pl.loop(0, bx)
        def _(x):
            beyond = zero
            for y in range(by):
                v = p[k, x + 1, y + 1]
                near = (p[k, x, y + 1], p[k, x + 2, y + 1], p[k, x + 1, y], p[k, x + 1, y + 2],
                        pltpu.roll(v, 1, 1), pltpu.roll(v, LANES - 1, 1))
                w = [spread(wgt, i, x, pl.ds(y, 1)) for i in range(7)]
                t = [w[i] * near[i] for i in range(6)]
                v = w[6] * v - (((t[0] + t[1]) + (t[2] + t[3])) + (t[4] + t[5]))
                p[k + 1, x + 1, y + 1] = v
                if k < BASIS - 1:
                    beyond = jnp.where(inject(y), pltpu.roll(v, (8 * y + 4) % LANES, 1), beyond)
            if k < BASIS - 1:
                inj[k + 1, x] = beyond

    def rim_edges(k):
        for side in range(2):
            low, high = zero, zero
            for x in range(bx):
                v = e[k, x + 1, side]
                here = (lane >> 3) == x
                low = jnp.where(here, pltpu.roll(v, 8 * x, 1) if x else v, low)
                high = jnp.where(here, pltpu.roll(v, (8 * x + 8) % LANES, 1), high)
            yes[k, 0, side] = low
            yes[k, 1, side] = high

    def rim_step(k):
        for side in range(2):
            before, after = yer[k, 0, side], yer[k, 1, side]
            low, high = zero, zero
            for x in range(bx):
                v = e[k, x + 1, side]
                beyond = inj[k, x]
                ym = jnp.where(lane < 8, pltpu.roll(before, (LANES - 8 * x) % LANES, 1), pltpu.roll(v, 8, 1))
                yp = jnp.where(lane >= LANES - 8, pltpu.roll(after, LANES - 8 - 8 * x, 1), pltpu.roll(v, LANES - 8, 1))
                zm = pltpu.roll(jnp.where(place == 7, beyond, v) if side else v, 1, 1)
                zp = pltpu.roll(v if side else jnp.where(place == 0, beyond, v), LANES - 1, 1)
                near = (e[k, x, side], e[k, x + 2, side], ym, yp, zm, zp)
                w = [spread(wge, i, side, pl.ds(x, 1)) for i in range(7)]
                t = [w[i] * near[i] for i in range(6)]
                v = w[6] * v - (((t[0] + t[1]) + (t[2] + t[3])) + (t[4] + t[5]))
                e[k + 1, x + 1, side] = v
                if k < BASIS - 1:
                    here = (lane >> 3) == x
                    low = jnp.where(here, pltpu.roll(v, 8 * x, 1) if x else v, low)
                    high = jnp.where(here, pltpu.roll(v, (8 * x + 8) % LANES, 1), high)
            if k < BASIS - 1:
                yes[k + 1, 0, side] = low
                yes[k + 1, 1, side] = high

    start(far())
    start(far_coefficient())
    start(field(0))
    start(coefficient())
    moments(0)

    arrive(coefficient())

    @pl.loop(0, bx)
    def _(x):
        c = eps[pl.ds(x * by, by), :]
        ey[x, pl.ds(0, 8), :] = spread(ey, bx, pl.ds(8 + x, 1))
        ey[x, pl.ds(8 + by, 8), :] = spread(ey, bx + 1, pl.ds(8 + x, 1))
        total = scr[pl.ds(x * by, by), :] * 0.02 - 0.4
        near = (ex[x], ex[x + 2], ey[x, pl.ds(7, by), :], ey[x, pl.ds(9, by), :],
                pltpu.roll(c, 1, 1), pltpu.roll(c, LANES - 1, 1))
        for i, n in enumerate(near):
            w = (c + n) * 0.01
            wgt[i, x] = w
            total = total + w
        wgt[6, x] = total

    arrive(field(0))
    step(0)
    start(field(1))
    moments(1)
    arrive(field(1))
    step(1)
    start(field(2))

    arrive(far())
    arrive(far_coefficient())

    @pl.loop(0, bx // 2)
    def _(j):
        even, odd = e[0, 2 * j + 1, 0], e[0, 2 * j + 2, 0]
        lo, hi = rup[0, j], rup[1, j]
        e[0, 2 * j + 1, 0] = jnp.where(place < 4, lo, even)
        e[0, 2 * j + 2, 0] = jnp.where(place < 4, pltpu.roll(lo, LANES - 4, 1), odd)
        e[0, 2 * j + 1, 1] = jnp.where(place < 4, even, pltpu.roll(hi, 4, 1))
        e[0, 2 * j + 2, 1] = jnp.where(place < 4, odd, hi)

    rim_edges(0)
    c_e, c_s = ce[0], ce[1]
    e_side = (jnp.where(place_e < 4, crecv[0], c_e), jnp.where(place_e < 4, c_e, crecv[1]))
    s_side = (jnp.where(place_e < 4, pltpu.roll(crecv[0], LANES - 4, 1), c_s),
              jnp.where(place_e < 4, c_s, pltpu.roll(crecv[1], 4, 1)))
    ees[0] = e_side[0]
    ees[1] = e_side[1]
    start(rim_coefficient())
    start(rim(0))

    moments(2)
    arrive(field(2))
    step(2)
    start(field(3))

    arrive(rim_coefficient())
    for side in range(2):
        c, beyond = ees[side], ie[...]
        xm = jnp.where(row_e == 0, pltpu.roll(eer[0, side], 1, 0), pltpu.roll(c, 1, 0))
        xp = jnp.where(row_e == bx - 1, pltpu.roll(eer[1, side], bx - 1, 0), pltpu.roll(c, bx - 1, 0))
        ym = jnp.where(lane_e < 8, pltpu.roll(eer[2, side], 8, 1), pltpu.roll(c, 8, 1))
        yp = jnp.where(lane_e >= LANES - 8, pltpu.roll(eer[3, side], LANES - 8, 1), pltpu.roll(c, LANES - 8, 1))
        zm = pltpu.roll(jnp.where(place_e == 7, beyond, c) if side else c, 1, 1)
        zp = pltpu.roll(c if side else jnp.where(place_e == 0, beyond, c), LANES - 1, 1)
        if side:
            inside = (place_e < 4) | (iz < nz - 1)
        else:
            inside = (place_e >= 4) | (iz > 0)
        total = s_side[side] * 0.02 - 0.4
        for i, n in enumerate((xm, xp, ym, yp, zm, zp)):
            w = (c + n) * 0.01
            wge[i, side] = jnp.where(inside, w, 0.0)
            total = total + w
        wge[6, side] = jnp.where(inside, total, 0.0)

    arrive(rim(0))
    rim_step(0)
    start(rim(1))
    arrive(field(3))
    step(3)
    arrive(rim(1))
    rim_step(1)
    start(rim(2))
    moments(3)
    arrive(rim(2))
    rim_step(2)
    start(rim(3))
    moments(4)
    for k in range(BASIS):
        rim_moments(k)
    table = reduce(0, 2 * BASIS - 1, zero)
    arrive(rim(3))
    rim_step(3)
    rim_moments(BASIS)
    total = reduce(2 * BASIS - 1, MOMENTS, table)

    for stage, (n, peer, me, slots, send, recv) in enumerate((
        (nx, peer1, ix, r1, as1, ar1), (nz // 2, peer2, zx, r2, as2, ar2), (n3, peer3, me3, r3, as3, ar3))):
        sbuf[stage] = total
        slots[me] = total

        def copy(d, mine):
            j, device = peer(d)
            return pltpu.make_async_remote_copy(
                src_ref=sbuf.at[stage], dst_ref=slots.at[me if mine else j], send_sem=send.at[d],
                recv_sem=recv.at[me if mine else j], device_id=device, device_id_type=MESH)

        @pl.loop(1, n)
        def _(d):
            copy(d, True).start()

        if stage == 0:
            for k in range(BASIS):
                sent(field(k))
                sent(rim(k))
            for c in (far(), far_coefficient(), coefficient(), rim_coefficient()):
                sent(c)

        if stage == 2:
            @pl.loop(0, bx)
            def _(x):
                border = jnp.where(place < 4, e[BASIS, x + 1, 1], e[BASIS, x + 1, 0])
                inner = (lane >= BASIS) & (lane < LANES - BASIS)
                for y in range(by):
                    v = jnp.where(inner, p[BASIS, x + 1, y + 1], pltpu.roll(border, (LANES - 4 - 8 * y) % LANES, 1))
                    top[pl.ds(x * by + y, 8, stride=bx * by), :] = v

        @pl.loop(1, n)
        def _(d):
            copy(d, False).wait_recv()
        parts = [slots[j] for j in range(n)]
        while len(parts) > 1:
            parts = [parts[i] + parts[i + 1] for i in range(0, len(parts) - 1, 2)] + ([parts[-1]] if len(parts) % 2 else [])
        total = parts[0]

        @pl.loop(1, n)
        def _(d):
            copy(d, True).wait_send()

    cells = bx * by * LANES * nx * ny * nz
    total = total * (1.0 / cells)
    for i in range(BASIS + 1):
        gram[pl.ds(8 * i, 8), :] = total if i == 0 else pltpu.roll(total, LANES - 8 * i, 1)


def per_device(sizes, charges, permittivity, screening):
    _, bx, by, bz = charges.shape
    nx, ny, nz = sizes
    dims = (bx, by, nx, ny, nz)
    vmem = pl.BlockSpec(memory_space=pltpu.VMEM)
    dma = pltpu.SemaphoreType.DMA

    def buf(*shape):
        return pltpu.VMEM(shape, F32)

    tile = (8, LANES)
    top, gram = pl.pallas_call(
        functools.partial(kernel, dims),
        out_shape=(
            jax.ShapeDtypeStruct((NRHS * bx * by, bz), F32),
            jax.ShapeDtypeStruct((8 * (BASIS + 1), LANES), F32),
        ),
        in_specs=[vmem] * 3,
        out_specs=(vmem, vmem),
        scratch_shapes=[
            buf(BASIS + 1, bx + 2, by + 2, *tile),
            buf(bx + 2, by, LANES),
            buf(bx + 2, by + 16, LANES),
            buf(2, bx, LANES),
            buf(7, bx, by, LANES),
            buf(BASIS + 1, bx + 2, 2, *tile),
            buf(BASIS, bx, *tile),
            buf(BASIS, 2, 2, *tile), buf(BASIS, 2, 2, *tile),
            buf(2, bx // 2, *tile), buf(2, bx // 2, *tile),
            buf(2, bx, LANES), buf(bx, LANES),
            buf(2, bx, LANES), buf(2, bx, LANES),
            buf(2, bx, LANES), buf(4, 2, bx, LANES),
            buf(7, 2, bx, LANES),
            buf(MOMENTS, 5, *tile),
            buf(3, *tile), buf(nx, *tile), buf(nz // 2, *tile), buf(2 * ny, *tile),
            dma((BASIS, 4)), dma((BASIS, 4)), dma((BASIS, 4)), dma((BASIS, 4)),
            dma((2,)), dma((2,)), dma((2,)), dma((2,)), dma((4,)), dma((4,)), dma((4,)), dma((4,)),
            dma((nx,)), dma((nx,)), dma((nz // 2,)), dma((nz // 2,)), dma((2 * ny,)), dma((2 * ny,)),
        ],
        compiler_params=pltpu.CompilerParams(collective_id=0, has_side_effects=True),
    )(charges.reshape(NRHS * bx * by, bz), permittivity.reshape(bx * by, bz), screening.reshape(bx * by, bz))
    columns = NRHS * (BASIS + 1)
    r_factor = jnp.linalg.cholesky(gram[:, :columns]).T
    return top.reshape(NRHS, bx, by, bz), r_factor


def solution(mesh):
    sizes = tuple(mesh.shape[a] for a in ("gx", "gy", "gz"))
    placed = (P(None, "gx", "gy", "gz"), P("gx", "gy", "gz"), P("gx", "gy", "gz"))
    return jax.shard_map(
        functools.partial(per_device, sizes),
        mesh=mesh,
        in_specs=placed,
        out_specs=(P(None, "gx", "gy", "gz"), P()),
        check_vma=False,
    )
```

time: 100 us -> 85.4 us (0.85)
  Pallas kernels: 90.7 us -> 75.6 us
    pallas_call x1, Pallas kernels: 90.7 us -> 75.6 us  [per_device(): pl.pallas_call(functools.partial(kernel, dims), out_shape=(jax.ShapeDtype...]
where the time goes in v2:
time: 85.4 us; the launch traced here: 85.1 us
  Pallas kernels  75.6 us (89%)
  other arithmetic  4.98 us (6%)
  local copies, waits for them, and re-layouts  3.85 us (5%)
    pallas_call x1, Pallas kernels, per_device(): pl.pallas_call(functools.partial(kernel, dims), out_shape=(jax.ShapeDtype...  75.6 us
    another operation x3, other arithmetic, per_device(): r_factor = jnp.linalg.cholesky(gram[:, :columns]).T  4.33 us
    unnamed x2, local copies, waits for them, and re-layouts  2.95 us

profile of v2, /device:TPU:1, one launch (start us, length us, event | category | flops | bytes accessed | tf_op | source)
XLA Modules:
  0.0 85.1 jit_solution(15996817809869158390)
XLA Ops:
  0.6 75.6 %shard_map.50 = (f32[2048,128]{1,0:T(8,128)}, f32[40,128]{1,0:T(8,128)}) custom-call(f32[2048,128]{1,0:T(8,128)} %bitcast.10, f32[256,128]{1,0:T(8,128)} %bitcast.12, f32[256,128]{1,0:T(8,128)} %bitcast.13), custom_call_target="tpu_custom_call" | custom-call | tf_op jit(solution)/shard_map/pallas_call | solution.py:467
  76.3 0.8 copy.5
  77.1 0.1 copy.6
  77.2 3.6 %cholesky.18 = f32[40,40]{1,0:T(8,128)S(1)} custom-call(f32[40,40]{1,0:T(8,128)S(1)} %fusion), custom_call_target="Cholesky" | custom-call | tf_op jit(solution)/shard_map/jit(cholesky)/cholesky | solution.py:498
  80.9 0.6 compare_reduce_fusion
  81.5 0.7 select_bitcast_fusion
  82.2 0.7 copy.7
  82.8 2.3 %copy.9 = f32[8,16,16,128]{3,2,1,0:T(8,128)} copy(f32[8,16,16,128]{3,2,1,0:T(8,128)} %bitcast.11) | data formatting | bytes 2097152
  (3 shorter events, 0.0 us)

commit v3 on v2

--- a/solution.py
+++ b/solution.py
@@ -19,7 +19,7 @@
     return lax.broadcasted_iota(jnp.int32, (8, LANES), dim)
 
 
-def kernel(dims, ch, eps, scr, top, gram, p, ex, ey, eys, wgt, e, inj, yes, yer, sup, rup,
+def kernel(dims, ch_in, eps_in, scr_in, top, gram, ch, eps, scr, insem, p, ex, ey, eys, wgt, e, inj, yes, yer, sup, rup,
            ce, ie, csend, crecv, ees, eer, wge, acc, sbuf, r1, r2, r3,
            ssem, rsem, xsem, ysem, zsem, tsem, usem, vsem, esem, fsem, gsem, hsem,
            as1, ar1, as2, ar2, as3, ar3):
@@ -55,18 +55,26 @@
         h = lax.div(j, ny)
         return j, (ix, j - h * ny, 2 * zx + h)
 
+    loads = [pltpu.make_async_copy(src, dst, insem.at[i])
+             for i, (src, dst) in enumerate(((ch_in, ch), (eps_in, eps), (scr_in, scr)))]
+    for c in loads:
+        c.start()
+
     barrier = pltpu.get_barrier_semaphore()
     count = jnp.int32(0)
-    for out, peer, _ in faces:
+    for out, peer, _ in faces[4:]:
         @pl.when(out)
         def _():
             pl.semaphore_signal(barrier, inc=1, device_id=peer, device_id_type=MESH)
         count = count + jnp.where(out, 1, 0)
-    for n, peer in ((nx, peer1), (nz // 2, peer2), (n3, peer3)):
+    for n, peer in ((n3, peer3), (nx, peer1), (nz // 2, peer2)):
         @pl.loop(1, n)
         def _(d):
             pl.semaphore_signal(barrier, inc=1, device_id=peer(d)[1], device_id_type=MESH)
         count = count + (n - 1)
+
+    for c in loads:
+        c.wait()
 
     def inject(y):
         return (lane == (8 * y + 8) % LANES) | (lane == (8 * y - 1) % LANES)
@@ -254,22 +262,35 @@
     def spread(ref, *at):
         return jnp.broadcast_to(ref[at], (8, LANES))
 
-    def step(k):
-        @pl.loop(0, bx)
+    def cells(k, x, ys, beyond):
+        for y in ys:
+            v = p[k, x + 1, y + 1]
+            near = (p[k, x, y + 1], p[k, x + 2, y + 1], p[k, x + 1, y], p[k, x + 1, y + 2],
+                    pltpu.roll(v, 1, 1), pltpu.roll(v, LANES - 1, 1))
+            w = [spread(wgt, i, x, pl.ds(y, 1)) for i in range(7)]
+            t = [w[i] * near[i] for i in range(6)]
+            v = w[6] * v - (((t[0] + t[1]) + (t[2] + t[3])) + (t[4] + t[5]))
+            p[k + 1, x + 1, y + 1] = v
+            if k < BASIS - 1:
+                beyond = jnp.where(inject(y), pltpu.roll(v, (8 * y + 4) % LANES, 1), beyond)
+        if k < BASIS - 1:
+            inj[k + 1, x] = beyond
+
+    def interior(k):
+        @pl.loop(1, bx - 1)
         def _(x):
-            beyond = zero
-            for y in range(by):
-                v = p[k, x + 1, y + 1]
-                near = (p[k, x, y + 1], p[k, x + 2, y + 1], p[k, x + 1, y], p[k, x + 1, y + 2],
-                        pltpu.roll(v, 1, 1), pltpu.roll(v, LANES - 1, 1))
-                w = [spread(wgt, i, x, pl.ds(y, 1)) for i in range(7)]
-                t = [w[i] * near[i] for i in range(6)]
-                v = w[6] * v - (((t[0] + t[1]) + (t[2] + t[3])) + (t[4] + t[5]))
-                p[k + 1, x + 1, y + 1] = v
-                if k < BASIS - 1:
-                    beyond = jnp.where(inject(y), pltpu.roll(v, (8 * y + 4) % LANES, 1), beyond)
-            if k < BASIS - 1:
-                inj[k + 1, x] = beyond
+            cells(k, x, range(1, by - 1), zero)
+
+    def border(k):
+        @pl.loop(0, 2)
+        def _(j):
+            cells(k, j * (bx - 1), range(by), zero)
+
+        @pl.loop(0, 2)
+        def _(j):
+            for i in range(bx // 2 - 1):
+                x = 1 + j * (bx // 2 - 1) + i
+                cells(k, x, (0, by - 1), inj[k + 1, x] if k < BASIS - 1 else zero)
 
     def rim_edges(k):
         for side in range(2):
@@ -306,10 +327,10 @@
                 yes[k + 1, 0, side] = low
                 yes[k + 1, 1, side] = high
 
+    start(coefficient())
     start(far())
     start(far_coefficient())
     start(field(0))
-    start(coefficient())
     moments(0)
 
     arrive(coefficient())
@@ -328,13 +349,16 @@
             total = total + w
         wgt[6, x] = total
 
+    interior(0)
     arrive(field(0))
-    step(0)
+    border(0)
     start(field(1))
+    interior(1)
     moments(1)
     arrive(field(1))
-    step(1)
+    border(1)
     start(field(2))
+    interior(2)
 
     arrive(far())
     arrive(far_coefficient())
@@ -357,11 +381,7 @@
     ees[1] = e_side[1]
     start(rim_coefficient())
     start(rim(0))
-
     moments(2)
-    arrive(field(2))
-    step(2)
-    start(field(3))
 
     arrive(rim_coefficient())
     for side in range(2):
@@ -386,15 +406,19 @@
     arrive(rim(0))
     rim_step(0)
     start(rim(1))
-    arrive(field(3))
-    step(3)
+    arrive(field(2))
+    border(2)
+    start(field(3))
     arrive(rim(1))
     rim_step(1)
     start(rim(2))
+    interior(3)
     moments(3)
     arrive(rim(2))
     rim_step(2)
     start(rim(3))
+    arrive(field(3))
+    border(3)
     moments(4)
     for k in range(BASIS):
         rim_moments(k)
@@ -470,9 +494,11 @@
             jax.ShapeDtypeStruct((NRHS * bx * by, bz), F32),
             jax.ShapeDtypeStruct((8 * (BASIS + 1), LANES), F32),
         ),
-        in_specs=[vmem] * 3,
+        in_specs=[pl.BlockSpec(memory_space=pltpu.HBM)] * 3,
         out_specs=(vmem, vmem),
         scratch_shapes=[
+            buf(NRHS * bx * by, LANES), buf(bx * by, LANES), buf(bx * by, LANES),
+            dma((3,)),
             buf(BASIS + 1, bx + 2, by + 2, *tile),
             buf(bx + 2, by, LANES),
             buf(bx + 2, by + 16, LANES),
@@ -492,11 +518,11 @@
             dma((2,)), dma((2,)), dma((2,)), dma((2,)), dma((4,)), dma((4,)), dma((4,)), dma((4,)),
             dma((nx,)), dma((nx,)), dma((nz // 2,)), dma((nz // 2,)), dma((2 * ny,)), dma((2 * ny,)),
         ],
-        compiler_params=pltpu.CompilerParams(collective_id=0, has_side_effects=True),
+        compiler_params=pltpu.CompilerParams(collective_id=0, has_side_effects=True, vmem_limit_bytes=(64 << 20) - 2600000),
     )(charges.reshape(NRHS * bx * by, bz), permittivity.reshape(bx * by, bz), screening.reshape(bx * by, bz))
     columns = NRHS * (BASIS + 1)
-    r_factor = jnp.linalg.cholesky(gram[:, :columns]).T
-    return top.reshape(NRHS, bx, by, bz), r_factor
+    lower = lax.linalg.cholesky(gram[:, :columns], symmetrize_input=False)
+    return top.reshape(NRHS, bx, by, bz), lower.T
 
 
 def solution(mesh):

time: 85.4 us -> 77.4 us (0.906)
  Pallas kernels: 75.6 us -> 67.9 us
  local copies, waits for them, and re-layouts: 3.85 us -> 2.95 us
    pallas_call x1, Pallas kernels: 75.6 us -> 67.9 us  [per_device(): pl.pallas_call(functools.partial(kernel, dims), out_shape=(jax.ShapeDtype...]
where the time goes in v3:
time: 77.4 us; the launch traced here: 77.2 us
  Pallas kernels  67.9 us (88%)
  other arithmetic  5.69 us (7%)
  local copies, waits for them, and re-layouts  2.95 us (4%)
    pallas_call x1, Pallas kernels, per_device(): pl.pallas_call(functools.partial(kernel, dims), out_shape=(jax.ShapeDtype...  67.9 us
    another operation x3, other arithmetic, per_device(): lower = lax.linalg.cholesky(gram[:, :columns], symmetrize_input=False)  5.04 us
    unnamed x2, local copies, waits for them, and re-layouts  2.95 us

profile of v3, /device:TPU:1, one launch (start us, length us, event | category | flops | bytes accessed | tf_op | source)
XLA Modules:
  0.0 77.2 jit_solution(14864412586552421759)
XLA Ops:
  0.6 67.9 %shard_map.50 = (f32[2048,128]{1,0:T(8,128)}, f32[40,128]{1,0:T(8,128)}) custom-call(f32[2048,128]{1,0:T(8,128)} %bitcast.7, f32[256,128]{1,0:T(8,128)} %bitcast.9, f32[256,128]{1,0:T(8,128)} %bitcast.10), custom_call_target="tpu_custom_call" | custom-call | tf_op jit(solution)/shard_map/pallas_call | solution.py:491
  68.5 4.4 %cholesky.32 = f32[40,40]{1,0:T(8,128)S(1)} custom-call(f32[40,40]{1,0:T(8,128)} %bitcast.11), custom_call_target="Cholesky" | custom-call | tf_op jit(solution)/shard_map/cholesky | solution.py:524
  72.9 0.6 compare_reduce_fusion
  73.6 0.7 select_bitcast_fusion
  74.2 0.7 copy.5
  74.9 2.3 %copy.7 = f32[8,16,16,128]{3,2,1,0:T(8,128)} copy(f32[8,16,16,128]{3,2,1,0:T(8,128)} %bitcast.8) | data formatting | bytes 2097152
  (1 shorter events, 0.0 us)

commit v4 on v3

--- a/solution.py
+++ b/solution.py
@@ -19,7 +19,7 @@
     return lax.broadcasted_iota(jnp.int32, (8, LANES), dim)
 
 
-def kernel(dims, ch_in, eps_in, scr_in, top, gram, ch, eps, scr, insem, p, ex, ey, eys, wgt, e, inj, yes, yer, sup, rup,
+def kernel(dims, ch_in, eps_in, scr_in, top_out, gram, ch, eps, scr, top, insem, p, ex, ey, eys, wgt, e, inj, yes, yer, sup, rup,
            ce, ie, csend, crecv, ees, eer, wge, acc, sbuf, r1, r2, r3,
            ssem, rsem, xsem, ysem, zsem, tsem, usem, vsem, esem, fsem, gsem, hsem,
            as1, ar1, as2, ar2, as3, ar3):
@@ -328,9 +328,9 @@
                 yes[k + 1, 1, side] = high
 
     start(coefficient())
+    start(field(0))
     start(far())
     start(far_coefficient())
-    start(field(0))
     moments(0)
 
     arrive(coefficient())
@@ -428,6 +428,7 @@
     rim_moments(BASIS)
     total = reduce(2 * BASIS - 1, MOMENTS, table)
 
+    store = pltpu.make_async_copy(top, top_out, insem.at[3])
     for stage, (n, peer, me, slots, send, recv) in enumerate((
         (nx, peer1, ix, r1, as1, ar1), (nz // 2, peer2, zx, r2, as2, ar2), (n3, peer3, me3, r3, as3, ar3))):
         sbuf[stage] = total
@@ -458,6 +459,7 @@
                 for y in range(by):
                     v = jnp.where(inner, p[BASIS, x + 1, y + 1], pltpu.roll(border, (LANES - 4 - 8 * y) % LANES, 1))
                     top[pl.ds(x * by + y, 8, stride=bx * by), :] = v
+            store.start()
 
         @pl.loop(1, n)
         def _(d):
@@ -471,6 +473,7 @@
         def _(d):
             copy(d, True).wait_send()
 
+    store.wait()
     cells = bx * by * LANES * nx * ny * nz
     total = total * (1.0 / cells)
     for i in range(BASIS + 1):
@@ -495,10 +498,11 @@
             jax.ShapeDtypeStruct((8 * (BASIS + 1), LANES), F32),
         ),
         in_specs=[pl.BlockSpec(memory_space=pltpu.HBM)] * 3,
-        out_specs=(vmem, vmem),
+        out_specs=(pl.BlockSpec(memory_space=pltpu.HBM), vmem),
         scratch_shapes=[
             buf(NRHS * bx * by, LANES), buf(bx * by, LANES), buf(bx * by, LANES),
-            dma((3,)),
+            buf(NRHS * bx * by, LANES),
+            dma((4,)),
             buf(BASIS + 1, bx + 2, by + 2, *tile),
             buf(bx + 2, by, LANES),
             buf(bx + 2, by + 16, LANES),
@@ -518,11 +522,26 @@
             dma((2,)), dma((2,)), dma((2,)), dma((2,)), dma((4,)), dma((4,)), dma((4,)), dma((4,)),
             dma((nx,)), dma((nx,)), dma((nz // 2,)), dma((nz // 2,)), dma((2 * ny,)), dma((2 * ny,)),
         ],
-        compiler_params=pltpu.CompilerParams(collective_id=0, has_side_effects=True, vmem_limit_bytes=(64 << 20) - 2600000),
+        compiler_params=pltpu.CompilerParams(collective_id=0, has_side_effects=True, vmem_limit_bytes=(64 << 20) - 9000000),
     )(charges.reshape(NRHS * bx * by, bz), permittivity.reshape(bx * by, bz), screening.reshape(bx * by, bz))
     columns = NRHS * (BASIS + 1)
     lower = lax.linalg.cholesky(gram[:, :columns], symmetrize_input=False)
-    return top.reshape(NRHS, bx, by, bz), lower.T
+    top, r_factor = pl.pallas_call(
+        finish,
+        out_shape=(
+            jax.ShapeDtypeStruct((NRHS * bx * by, bz), F32),
+            jax.ShapeDtypeStruct((columns, columns), F32),
+        ),
+        in_specs=[vmem] * 2,
+        out_specs=(vmem, vmem),
+        compiler_params=pltpu.CompilerParams(vmem_limit_bytes=8 << 20),
+    )(top, lower)
+    return top.reshape(NRHS, bx, by, bz), r_factor
+
+
+def finish(top_in, lower, top, r_factor):
+    top[...] = top_in[...]
+    r_factor[...] = lower[...].T
 
 
 def solution(mesh):

time: 77.4 us -> 73.8 us (0.953)
  Pallas kernels: 67.9 us -> 65.9 us
  local copies, waits for them, and re-layouts: 2.95 us -> 1.22 us
    pallas_call x1, Pallas kernels: 67.9 us -> 64.9 us  [per_device(): pl.pallas_call(functools.partial(kernel, dims), out_shape=(jax.ShapeDtype...]
    unnamed x2, local copies, waits for them, and re-layouts: 2.95 us -> 1.22 us
    pallas_call x0 -> x1, Pallas kernels: none -> 1.04 us  [per_device(): pl.pallas_call(finish, out_shape=(jax.ShapeDtypeStruct((NRHS * bx * by, b...]
where the time goes in v4:
time: 73.8 us; the launch traced here: 73.5 us
  Pallas kernels  65.9 us (89%)
  other arithmetic  5.69 us (8%)
  local copies, waits for them, and re-layouts  1.22 us (2%)
    pallas_call x1, Pallas kernels, per_device(): pl.pallas_call(functools.partial(kernel, dims), out_shape=(jax.ShapeDtype...  64.9 us
    another operation x3, other arithmetic, per_device(): lower = lax.linalg.cholesky(gram[:, :columns], symmetrize_input=False)  5.04 us

profile of v4, /device:TPU:1, one launch (start us, length us, event | category | flops | bytes accessed | tf_op | source)
XLA Modules:
  0.0 73.5 jit_solution(6024528865693472960)
XLA Ops:
  0.6 64.9 %shard_map.50 = (f32[2048,128]{1,0:T(8,128)}, f32[40,128]{1,0:T(8,128)}) custom-call(f32[2048,128]{1,0:T(8,128)} %bitcast.5, f32[256,128]{1,0:T(8,128)} %bitcast.6, f32[256,128]{1,0:T(8,128)} %bitcast.7), custom_call_target="tpu_custom_call" | custom-call | tf_op jit(solution)/shard_map/pallas_call | solution.py:494
  65.5 4.4 %cholesky.32 = f32[40,40]{1,0:T(8,128)S(1)} custom-call(f32[40,40]{1,0:T(8,128)} %bitcast.9), custom_call_target="Cholesky" | custom-call | tf_op jit(solution)/shard_map/cholesky | solution.py:528
  69.9 0.6 compare_reduce_fusion
  70.6 0.7 select_select_fusion.lower
  71.2 0.0 copy-start
  71.2 1.2 %copy-done = f32[2048,128]{1,0:T(8,128)S(1)} copy-done((f32[2048,128]{1,0:T(8,128)S(1)}, f32[2048,128]{1,0:T(8,128)}, u32[]{:S(2)}) %copy-start) | copy-done | bytes 1048600
  72.5 1.0 %shard_map.51 = (f32[2048,128]{1,0:T(8,128)}, f32[40,40]{1,0:T(8,128)}) custom-call(f32[2048,128]{1,0:T(8,128)S(1)} %copy-done, f32[40,40]{1,0:T(8,128)S(1)} %select_select_fusion.lower), custom_call_target="tpu_custom_call" | custom-call | tf_op jit(solution)/shard_map/pallas_call | solution.py:529
  (1 shorter events, 0.0 us)
Async XLA Ops:
  71.2 1.2 %copy-start = (f32[2048,128]{1,0:T(8,128)S(1)}, f32[2048,128]{1,0:T(8,128)}, u32[]{:S(2)}) copy-start(f32[2048,128]{1,0:T(8,128)} %get-tuple-element.6.top_in) | copy-start | bytes 3145732

commit v5 on v4

--- a/solution.py
+++ b/solution.py
@@ -381,8 +381,10 @@
     ees[1] = e_side[1]
     start(rim_coefficient())
     start(rim(0))
-    moments(2)
-
+
+    arrive(field(2))
+    border(2)
+    start(field(3))
     arrive(rim_coefficient())
     for side in range(2):
         c, beyond = ees[side], ie[...]
@@ -406,9 +408,7 @@
     arrive(rim(0))
     rim_step(0)
     start(rim(1))
-    arrive(field(2))
-    border(2)
-    start(field(3))
+    moments(2)
     arrive(rim(1))
     rim_step(1)
     start(rim(2))

time: 73.8 us -> 73.8 us (level)
  no operation moved by 1% of the time
where the time goes in v5:
time: 73.8 us; the launch traced here: 73.5 us
  Pallas kernels  65.9 us (89%)
  other arithmetic  5.69 us (8%)
  local copies, waits for them, and re-layouts  1.22 us (2%)
    pallas_call x1, Pallas kernels, per_device(): pl.pallas_call(functools.partial(kernel, dims), out_shape=(jax.ShapeDtype...  64.9 us
    another operation x3, other arithmetic, per_device(): lower = lax.linalg.cholesky(gram[:, :columns], symmetrize_input=False)  5.04 us

profile of v5, /device:TPU:1, one launch (start us, length us, event | category | flops | bytes accessed | tf_op | source)
XLA Modules:
  0.0 73.5 jit_solution(5454363011592707970)
XLA Ops:
  0.6 64.9 %shard_map.50 = (f32[2048,128]{1,0:T(8,128)}, f32[40,128]{1,0:T(8,128)}) custom-call(f32[2048,128]{1,0:T(8,128)} %bitcast.5, f32[256,128]{1,0:T(8,128)} %bitcast.6, f32[256,128]{1,0:T(8,128)} %bitcast.7), custom_call_target="tpu_custom_call" | custom-call | tf_op jit(solution)/shard_map/pallas_call | solution.py:494
  65.5 4.4 %cholesky.32 = f32[40,40]{1,0:T(8,128)S(1)} custom-call(f32[40,40]{1,0:T(8,128)} %bitcast.9), custom_call_target="Cholesky" | custom-call | tf_op jit(solution)/shard_map/cholesky | solution.py:528
  69.9 0.6 compare_reduce_fusion
  70.6 0.7 select_select_fusion.lower
  71.2 0.0 copy-start
  71.2 1.2 %copy-done = f32[2048,128]{1,0:T(8,128)S(1)} copy-done((f32[2048,128]{1,0:T(8,128)S(1)}, f32[2048,128]{1,0:T(8,128)}, u32[]{:S(2)}) %copy-start) | copy-done | bytes 1048600
  72.5 1.0 %shard_map.51 = (f32[2048,128]{1,0:T(8,128)}, f32[40,40]{1,0:T(8,128)}) custom-call(f32[2048,128]{1,0:T(8,128)S(1)} %copy-done, f32[40,40]{1,0:T(8,128)S(1)} %select_select_fusion.lower), custom_call_target="tpu_custom_call" | custom-call | tf_op jit(solution)/shard_map/pallas_call | solution.py:529
  (1 shorter events, 0.0 us)
Async XLA Ops:
  71.2 1.2 %copy-start = (f32[2048,128]{1,0:T(8,128)S(1)}, f32[2048,128]{1,0:T(8,128)}, u32[]{:S(2)}) copy-start(f32[2048,128]{1,0:T(8,128)} %get-tuple-element.6.top_in) | copy-start | bytes 3145732
